TPU v7x, 128 devices: a whole 4x4x4 slice. The times are simulated.
128 devices in a mesh: lat: 8 (over y, core), lon: 16 (over x, z).
Axes of the slice: x: 4, y: 4, z: 4, core: 2. Of those that a mesh axis runs over, the one named last changes fastest.
Arguments:
- obs_pert: bfloat16 [8192, 128, 256], P(('lat', 'lon')), may hold values from -4 to 4
- obs_dep: bfloat16 [8192, 128], P(('lat', 'lon')), may hold values from -6 to 6
- valid_rows: int32 [8192], P(('lat', 'lon')), may hold values from 1 to 128
- local_lists: int32 [512, 24], P(('lat', 'lon')), may hold values from 0 to 8191, as said below
- state_mean: float32 [8, 262144], P(None, ('lat', 'lon')), may hold values from -6 to 6
- state_pert: bfloat16 [8, 262144, 256], P(None, ('lat', 'lon')), may hold values from -6 to 6
- interp_lists: int32 [8192, 4], P(('lat', 'lon')), may hold values from 0 to 511, as said below
- interp_coef: float32 [4, 262144], P(None, ('lat', 'lon')), may hold values from 0.1 to 0.6
Outputs:
- analysis: bfloat16 [8, 262144, 256], P(None, ('lat', 'lon'))
Inputs may be any that keep to these rules, and one draw needn't show every extreme that they name: `local_lists`: device i of lat+lon stores blocks i * 64 to (i + 1) * 64 - 1. Among the lists of the 4 domains of one device, at most 2 entries name blocks stored on any one device, and on every owner some device serves exactly 2. Entries may repeat. `interp_lists`: domain g is owned by device g // 4 of lat+lon. Every domain named for a tile of device (a, b) is owned by a device whose lat index differs from a by at most 1 and whose lon index differs from b by at most 1 modulo the lon axis's size.
All inputs are finite; a program needn't handle non-finite values.
Results may differ from a plain program's by a relative error of at most 0.003.
Values may be sent and summed in bfloat16 or wider, within the bound.
A program may use at most 256 MiB of HBM per device.

v0:
```python
import jax
import jax.numpy as jnp
from jax import lax
from jax.sharding import PartitionSpec as P

NS_ITERS = 4


def with_halo(block, sides, width, periodic):
    for axis, dim in sides:
        count = lax.axis_size(axis)
        forward = [(i, i + 1) for i in range(count - 1)]
        if periodic:
            forward.append((count - 1, 0))
        backward = [(target, source) for source, target in forward]
        low = lax.ppermute(
            lax.slice_in_dim(block, block.shape[dim] - width, None, axis=dim), axis, forward
        )
        high = lax.ppermute(lax.slice_in_dim(block, 0, width, axis=dim), axis, backward)
        block = jnp.concatenate([low, block, high], axis=dim)
    return block


def make_weights(gram, innov, members):
    identity = jnp.eye(members, dtype=jnp.float32)
    system = (members - 1.0) * identity + gram
    scale = jnp.sqrt(jnp.sum(system * system, axis=(-2, -1)))[..., None, None]
    approx = system / scale
    inverse_root = jnp.broadcast_to(identity, system.shape)
    for sweep in range(NS_ITERS):
        factor = 1.5 * identity - 0.5 * jnp.matmul(
            inverse_root, approx, precision=lax.Precision.HIGHEST
        )
        approx = jnp.matmul(approx, factor, precision=lax.Precision.HIGHEST)
        inverse_root = jnp.matmul(factor, inverse_root, precision=lax.Precision.HIGHEST)
    inner = jnp.matmul(inverse_root, innov[..., None], precision=lax.Precision.HIGHEST)
    mean_weight = jnp.matmul(inverse_root, inner, precision=lax.Precision.HIGHEST) / scale
    return (jnp.sqrt((members - 1.0) / scale) * inverse_root + mean_weight).astype(jnp.bfloat16)


def local(
    obs_pert, obs_dep, valid_rows, local_lists, state_mean, state_pert, interp_lists, interp_coef
):
    n_devices = lax.axis_size(("lat", "lon"))
    n_lon = lax.axis_size("lon")
    blocks_here, block_rows, members = obs_pert.shape
    keep = jnp.arange(block_rows)[None, :] < valid_rows[:, None]
    masked_pert = jnp.where(keep[:, :, None], obs_pert, jnp.zeros((), jnp.bfloat16))
    masked_dep = jnp.where(keep, obs_dep, jnp.zeros((), jnp.bfloat16))
    capacity = 2 * max(1, 64 // n_devices)
    domains_here, list_len = local_lists.shape
    entries = local_lists.reshape(-1)
    source = entries // blocks_here
    local_index = entries % blocks_here
    onehot = (source[:, None] == jnp.arange(n_devices, dtype=jnp.int32)[None, :]).astype(jnp.int32)
    earlier = jnp.cumsum(onehot, axis=0) - onehot
    slot = jnp.sum(earlier * onehot, axis=1)
    flat_slot = source * capacity + slot
    request = jnp.zeros((n_devices * capacity,), jnp.int32).at[flat_slot].set(local_index)
    asked = lax.all_to_all(
        request.reshape(n_devices, capacity),
        ("lat", "lon"),
        split_axis=0,
        concat_axis=0,
        tiled=True,
    ).reshape(-1)
    out_pert = masked_pert[asked].reshape(n_devices, capacity, block_rows, members)
    out_dep = masked_dep[asked].reshape(n_devices, capacity, block_rows)
    arrived = (
        lax.all_to_all(out_pert, ("lat", "lon"), split_axis=0, concat_axis=0, tiled=True),
        lax.all_to_all(out_dep, ("lat", "lon"), split_axis=0, concat_axis=0, tiled=True),
    )
    got_pert = (
        arrived[0]
        .reshape(-1, block_rows, members)[flat_slot]
        .reshape(domains_here, list_len, block_rows, members)
    )
    got_dep = (
        arrived[1].reshape(-1, block_rows)[flat_slot].reshape(domains_here, list_len, block_rows)
    )
    gram = jnp.einsum("dlri,dlrj->dij", got_pert, got_pert, preferred_element_type=jnp.float32)
    innov = jnp.einsum("dlri,dlr->di", got_pert, got_dep, preferred_element_type=jnp.float32)
    weights = make_weights(gram, innov, members)
    tiles_near = with_halo(weights[None, None], (("lon", 1),), 1, True)
    tiles_near = with_halo(tiles_near, (("lat", 0),), 1, False)
    flat_tiles = tiles_near.reshape(9 * domains_here, members, members)
    owner = interp_lists // domains_here
    within = interp_lists % domains_here
    lat_step = owner // n_lon - lax.axis_index("lat")
    lon_step = (owner % n_lon - lax.axis_index("lon") + 1) % n_lon - 1
    position = ((lat_step + 1) * 3 + lon_step + 1) * domains_here + within
    chosen = flat_tiles[position]
    levels, cols_here, _ = state_pert.shape
    tiles_here, n_interp = interp_lists.shape
    tile_cols = cols_here // tiles_here
    perturbed = state_pert.reshape(levels, tiles_here, tile_cols, members)
    coef_tiles = interp_coef.reshape(n_interp, tiles_here, tile_cols)
    total = state_mean.reshape(levels, tiles_here, tile_cols)[..., None]
    for corner in range(n_interp):
        product = jnp.einsum(
            "ltci,tij->ltcj", perturbed, chosen[:, corner], preferred_element_type=jnp.float32
        )
        total = total + coef_tiles[corner][None, :, :, None] * product
    return total.reshape(levels, cols_here, members).astype(jnp.bfloat16)


def solution(mesh):
    in_specs = (
        P(("lat", "lon"), None, None),
        P(("lat", "lon"), None),
        P(("lat", "lon")),
        P(("lat", "lon"), None),
        P(None, ("lat", "lon")),
        P(None, ("lat", "lon"), None),
        P(("lat", "lon"), None),
        P(None, ("lat", "lon")),
    )
    out_specs = P(None, ("lat", "lon"), None)
    return jax.shard_map(local, mesh=mesh, in_specs=in_specs, out_specs=out_specs, check_vma=False)
```

profile of v0, /device:TPU:10, one launch (start us, length us, event | category | flops | bytes accessed | tf_op | source)
XLA Modules:
  0.0 469.0 jit_solution(4969660402857432700)
XLA Ops:
  3.6 10.4 %all-to-all-start = ((s32[128,1,2]{2,1,0:T(1,128)}), s32[128,1,2]{2,1,0:T(1,128)S(1)}, u32[]{:S(2)}, u32[]{:S(2)}) async-start(s32[128,1,2]{2,1,0:T(1,128)} %bitcast.2), calls=%async_computation | async-start | bytes 131072 | tf_op jit(solution)/shard_map/all_to_all | solution.py:60
  15.6 6.7 %all-to-all-done = s32[128,1,2]{2,1,0:T(1,128)S(1)} async-done(((s32[128,1,2]{2,1,0:T(1,128)}), s32[128,1,2]{2,1,0:T(1,128)S(1)}, u32[]{:S(2)}, u32[]{:S(2)}) %all-to-all-start) | async-done | bytes 1056 | tf_op jit(solution)/shard_map/all_to_all | solution.py:60
  23.8 1.5 gather_fusion.2
  25.2 5.8 %all-to-all-start.2 = ((bf16[128,2,128]{2,1,0:T(2,128)(2,1)}), bf16[128,2,128]{2,1,0:T(2,128)(2,1)S(1)}, u32[]{:S(2)}, u32[]{:S(2)}) async-start(bf16[128,2,128]{2,1,0:T(2,128)(2,1)} %bitcast.9), calls=%async_computation.2 | async-start | bytes 131072 | tf_op jit(solution)/shard_map/all_to_all | solution.py:71
  31.0 5.2 %broadcast_select_fusion = bf16[64,128,256]{2,1,0:T(8,128)(2,1)} fusion(bf16[64,128,256]{2,1,0:T(8,128)(2,1)} %param.8, pred[64,128]{1,0:T(8,128)(4,1)S(1)} %iota_compare_fusion.2), kind=kLoop, calls=%fused_computation.24 | loop fusion | flops 2097152 | bytes 8396800 | tf_op jit(solution)/shard_map/jit(_where)/select_n | solution.py:48
  36.2 11.6 %gather_fusion = bf16[256,128,256]{2,1,0:T(8,128)(2,1)} fusion(bf16[64,128,256]{2,1,0:T(8,128)(2,1)} %broadcast_select_fusion, s32[1024]{0:T(1024)S(1)} %pad_clamp_fusion.2), kind=kCustom, calls=%fused_computation | custom fusion | bytes 33555456 | tf_op jit(solution)/shard_map/gather | solution.py:67
  47.8 10.2 %all-to-all-start.1 = ((bf16[128,2,128,256]{3,2,1,0:T(8,128)(2,1)}), bf16[128,2,128,256]{3,2,1,0:T(8,128)(2,1)}, u32[]{:S(2)}, u32[]{:S(2)}) async-start(bf16[128,2,128,256]{3,2,1,0:T(8,128)(2,1)} %bitcast.125), calls=%async_computation.1 | async-start | bytes 33554432 | tf_op jit(solution)/shard_map/all_to_all | solution.py:70
  58.8 231.2 %all-to-all-done.1 = bf16[128,2,128,256]{3,2,1,0:T(8,128)(2,1)} async-done(((bf16[128,2,128,256]{3,2,1,0:T(8,128)(2,1)}), bf16[128,2,128,256]{3,2,1,0:T(8,128)(2,1)}, u32[]{:S(2)}, u32[]{:S(2)}) %all-to-all-start.1) | async-done | bytes 16777248 | tf_op jit(solution)/shard_map/all_to_all | solution.py:70
  290.0 12.0 %gather_fusion.1 = bf16[96,128,256]{2,1,0:T(8,128)(2,1)} fusion(bf16[256,128,256]{2,1,0:T(8,128)(2,1)} %bitcast.5, s32[1024]{0:T(1024)S(1)} %pad_clamp_fusion.1), kind=kCustom, calls=%fused_computation.1 | custom fusion | bytes 12583296 | tf_op jit(solution)/shard_map/gather | solution.py:74
  302.0 6.9 %multiply_reduce_fusion = (f32[4]{0:T(128)S(1)}, f32[4,256,256]{2,1,0:T(8,128)S(1)}) fusion(bf16[4,24,128,256]{3,2,1,0:T(8,128)(2,1)} %bitcast.121, f32[256,256]{1,0:T(8,128)S(1)} %fusion.22), kind=kOutput, calls=%fused_computation.37 | convolution fusion | flops 1611399168 | bytes 7602192 | tf_op jit(solution)/shard_map/dlri,dlrj->dij/dot_general | solution.py:81
  308.9 1.2 fusion.14
  310.1 1.2 fusion.23
  312.4 1.2 fusion.13
  315.9 1.2 fusion.12
  317.1 1.2 fusion.49
  318.2 1.4 fusion.50
  320.6 1.2 fusion.11
  325.3 2.0 collective-permute-start
  327.4 11.3 %collective-permute-done.1 = bf16[1,1,4,256,256]{4,3,2,1,0:T(8,128)(2,1)S(1)} collective-permute-done((bf16[1,1,4,256,256]{4,3,2,1,0:T(8,128)(2,1)S(1)}, bf16[1,1,4,256,256]{4,3,2,1,0:T(8,128)(2,1)S(1)}, u32[]{:S(2)}, u32[]{:S(2)}) %collective-permute-start.1) | collective-permute-done | bytes 524320 | tf_op jit(solution)/shard_map/ppermute | solution.py:19
  338.7 2.2 collective-permute-done
  340.9 1.3 pad_maximum_fusion.1
  342.2 11.9 %collective-permute-start.3 = (bf16[1,3,4,256,256]{4,3,2,1,0:T(8,128)(2,1)}, bf16[1,3,4,256,256]{4,3,2,1,0:T(8,128)(2,1)S(1)}, u32[]{:S(2)}, u32[]{:S(2)}) collective-permute-start(bf16[1,3,4,256,256]{4,3,2,1,0:T(8,128)(2,1)} %pad_maximum_fusion.1), channel_id=1, source_target_pairs={{16,0},{32,16},{48,32},{64,48},{80,64},{96,80},{112,96},{17,1},{33... | collective-permute-start | bytes 4718600 | tf_op jit(solution)/shard_map/ppermute | solution.py:19
  354.1 1.9 collective-permute-start.2
  358.7 13.7 %collective-permute-done.3 = bf16[1,3,4,256,256]{4,3,2,1,0:T(8,128)(2,1)S(1)} collective-permute-done((bf16[1,3,4,256,256]{4,3,2,1,0:T(8,128)(2,1)}, bf16[1,3,4,256,256]{4,3,2,1,0:T(8,128)(2,1)S(1)}, u32[]{:S(2)}, u32[]{:S(2)}) %collective-permute-start.3) | collective-permute-done | bytes 1572896 | tf_op jit(solution)/shard_map/ppermute | solution.py:19
  372.4 3.8 collective-permute-done.2
  376.2 3.8 pad_maximum_fusion
  380.0 16.2 %gather_fusion.4 = bf16[256,256,256]{2,1,0:T(8,128)(2,1)} fusion(bf16[36,256,256]{2,1,0:T(8,128)(2,1)} %bitcast.116, s32[1024]{0:T(1024)S(1)} %pad_clamp_fusion), kind=kCustom, calls=%fused_computation.4 | custom fusion | bytes 67109888 | tf_op jit(solution)/shard_map/gather | solution.py:92
  396.2 12.9 %fusion.2 = f32[64,256,8,32]{1,3,2,0:T(8,128)} fusion(bf16[64,4,256,256]{3,2,1,0:T(8,128)(2,1)} %bitcast.117, bf16[8,64,32,256]{3,2,1,0:T(8,128)(2,1)} %bitcast.112), kind=kOutput, calls=%fused_computation.14 | convolution fusion | flops 2147483648 | bytes 33554432 | tf_op jit(solution)/shard_map/ltci,tij->ltcj/dot_general | solution.py:100
  409.0 12.8 %fusion.3 = f32[64,256,8,32]{1,3,2,0:T(8,128)} fusion(bf16[64,4,256,256]{3,2,1,0:T(8,128)(2,1)} %bitcast.118, bf16[8,64,32,256]{3,2,1,0:T(8,128)(2,1)} %bitcast.113), kind=kOutput, calls=%fused_computation.16 | convolution fusion | flops 2147483648 | bytes 33554432 | tf_op jit(solution)/shard_map/ltci,tij->ltcj/dot_general | solution.py:100
  421.8 12.9 %fusion.4 = f32[64,256,8,32]{1,3,2,0:T(8,128)} fusion(bf16[64,4,256,256]{3,2,1,0:T(8,128)(2,1)} %bitcast.119, bf16[8,64,32,256]{3,2,1,0:T(8,128)(2,1)} %bitcast.114), kind=kOutput, calls=%fused_computation.18 | convolution fusion | flops 2147483648 | bytes 33554432 | tf_op jit(solution)/shard_map/ltci,tij->ltcj/dot_general | solution.py:100
  434.7 25.7 %fusion = bf16[8,64,32,256]{3,2,0,1:T(8,128)(2,1)} fusion(f32[64,256,8,32]{1,3,2,0:T(8,128)} %fusion.2, f32[64,256,8,32]{1,3,2,0:T(8,128)} %fusion.3, f32[64,256,8,32]{1,3,2,0:T(8,128)} %fusion.4, f32[64,32]{1,0:T(8,128)S(1)} %mul.144, f32[64,32]{1,0:T(8,128)S(1)} %mul.140, f32[64,32]{1,0:T(8,128)S(1)} %mul.136, f32[64,32]{1,0:T(8,128)S(1)} %mul.117, ...), kind=kOutput, calls=%fused_computation.7 | convolution fusion | flops 2185232384 | bytes 75595776 | tf_op jit(solution)/shard_map/ltci,tij->ltcj/dot_general | solution.py:100
  460.4 8.2 %copy.39 = bf16[8,64,32,256]{3,2,1,0:T(8,128)(2,1)} copy(bf16[8,64,32,256]{3,2,0,1:T(8,128)(2,1)} %fusion) | data formatting | bytes 16777216 | tf_op jit(solution)/shard_map/convert_element_type | solution.py:104
  (57 shorter events, 17.7 us)
Async XLA Ops:
  3.6 18.6 %all-to-all-start = ((s32[128,1,2]{2,1,0:T(1,128)}), s32[128,1,2]{2,1,0:T(1,128)S(1)}, u32[]{:S(2)}, u32[]{:S(2)}) async-start(s32[128,1,2]{2,1,0:T(1,128)} %bitcast.2), calls=%async_computation | async-start | bytes 131072 | tf_op jit(solution)/shard_map/all_to_all | solution.py:60
  25.2 22.6 %all-to-all-start.2 = ((bf16[128,2,128]{2,1,0:T(2,128)(2,1)}), bf16[128,2,128]{2,1,0:T(2,128)(2,1)S(1)}, u32[]{:S(2)}, u32[]{:S(2)}) async-start(bf16[128,2,128]{2,1,0:T(2,128)(2,1)} %bitcast.9), calls=%async_computation.2 | async-start | bytes 131072 | tf_op jit(solution)/shard_map/all_to_all | solution.py:71
  47.8 242.1 %all-to-all-start.1 = ((bf16[128,2,128,256]{3,2,1,0:T(8,128)(2,1)}), bf16[128,2,128,256]{3,2,1,0:T(8,128)(2,1)}, u32[]{:S(2)}, u32[]{:S(2)}) async-start(bf16[128,2,128,256]{3,2,1,0:T(8,128)(2,1)} %bitcast.125), calls=%async_computation.1 | async-start | bytes 33554432 | tf_op jit(solution)/shard_map/all_to_all | solution.py:70
  313.5 6.1 %slice-start = ((s8[6291456]{0:T(1024)(128)(4,1)}), s8[4194304]{0:T(1024)(128)(4,1)S(1)}, s32[]{:S(2)}) async-start(s8[6291456]{0:T(1024)(128)(4,1)} %bitcast.122), calls=%async_computation.3 | async-start | bytes 8388608
  315.9 3.8 slice-start.1
  319.7 36.4 %copy-start.2 = (s32[64,4]{0,1:T(4,128)S(1)}, s32[64,4]{0,1:T(4,128)}, u32[]{:S(2)}) copy-start(s32[64,4]{0,1:T(4,128)} %param.14) | copy-start | bytes 3076
  319.7 36.6 %copy-start.1 = (f32[4,2048]{1,0:T(4,128)S(1)}, f32[4,2048]{1,0:T(4,128)}, u32[]{:S(2)}) copy-start(f32[4,2048]{1,0:T(4,128)} %param.15) | copy-start | bytes 98308
  320.6 36.1 %copy-start = (f32[8,2048]{1,0:T(8,128)S(1)}, f32[8,2048]{1,0:T(8,128)}, u32[]{:S(2)}) copy-start(f32[8,2048]{1,0:T(8,128)} %param.12) | copy-start | bytes 196612
  325.3 13.4 %collective-permute-start.1 = (bf16[1,1,4,256,256]{4,3,2,1,0:T(8,128)(2,1)S(1)}, bf16[1,1,4,256,256]{4,3,2,1,0:T(8,128)(2,1)S(1)}, u32[]{:S(2)}, u32[]{:S(2)}) collective-permute-start(bf16[1,1,4,256,256]{4,3,2,1,0:T(8,128)(2,1)S(1)} %fusion.16), channel_id=1, source_target_pairs={{1,0},{2,1},{3,2},{4,3},{5,4},{6,5},{7,6},{8,7},{9,8},{10,9},{11,1... | collective-permute-start | bytes 1572872 | tf_op jit(solution)/shard_map/ppermute | solution.py:19
  325.3 15.6 %collective-permute-start = (bf16[1,1,4,256,256]{4,3,2,1,0:T(8,128)(2,1)S(1)}, bf16[1,1,4,256,256]{4,3,2,1,0:T(8,128)(2,1)S(1)}, u32[]{:S(2)}, u32[]{:S(2)}) collective-permute-start(bf16[1,1,4,256,256]{4,3,2,1,0:T(8,128)(2,1)S(1)} %fusion.16), channel_id=1, source_target_pairs={{0,1},{1,2},{2,3},{3,4},{4,5},{5,6},{6,7},{7,8},{8,9},{9,10},{10,1... | collective-permute-start | bytes 1572872 | tf_op jit(solution)/shard_map/ppermute | solution.py:16
  342.2 30.1 %collective-permute-start.3 = (bf16[1,3,4,256,256]{4,3,2,1,0:T(8,128)(2,1)}, bf16[1,3,4,256,256]{4,3,2,1,0:T(8,128)(2,1)S(1)}, u32[]{:S(2)}, u32[]{:S(2)}) collective-permute-start(bf16[1,3,4,256,256]{4,3,2,1,0:T(8,128)(2,1)} %pad_maximum_fusion.1), channel_id=1, source_target_pairs={{16,0},{32,16},{48,32},{64,48},{80,64},{96,80},{112,96},{17,1},{33... | collective-permute-start | bytes 4718600 | tf_op jit(solution)/shard_map/ppermute | solution.py:19
  354.1 22.1 %collective-permute-start.2 = (bf16[1,3,4,256,256]{4,3,2,1,0:T(8,128)(2,1)}, bf16[1,3,4,256,256]{4,3,2,1,0:T(8,128)(2,1)}, u32[]{:S(2)}, u32[]{:S(2)}) collective-permute-start(bf16[1,3,4,256,256]{4,3,2,1,0:T(8,128)(2,1)} %pad_maximum_fusion.1), channel_id=1, source_target_pairs={{0,16},{16,32},{32,48},{48,64},{64,80},{80,96},{96,112},{1,17},{17... | collective-permute-start | bytes 4718600 | tf_op jit(solution)/shard_map/ppermute | solution.py:16
where the time goes:
time: 475 us; the launch traced here: 469 us
  waiting for transfers between devices  269 us (57%)
  matrix products  87 us (18%)
  local copies, waits for them, and re-layouts  56.4 us (12%)
  starting transfers between devices  42.3 us (9%)
  other arithmetic  13.6 us (3%)
    all_to_all x1, waiting for transfers between devices, local(): lax.all_to_all(out_pert, ('lat', 'lon'), split_axis=0, concat_axis=0, til...  231 us
    dot_general x4, matrix products, local(): jnp.einsum('ltci,tij->ltcj', perturbed, chosen[:, corner], preferred_elem...  64.2 us
    ppermute x2, waiting for transfers between devices, with_halo(): lax.ppermute(lax.slice_in_dim(block, 0, width, axis=dim), axis, backward)  25 us
    gather x1, local copies, waits for them, and re-layouts, local(): chosen = flat_tiles[position]  16.2 us
    ppermute x2, starting transfers between devices, with_halo(): lax.ppermute(lax.slice_in_dim(block, 0, width, axis=dim), axis, backward)  12 us
    gather x1, local copies, waits for them, and re-layouts, local(): arrived[0].reshape(-1, block_rows, members)[flat_slot]  12 us
    gather x1, local copies, waits for them, and re-layouts, local(): masked_pert[asked].reshape(n_devices, capacity, block_rows, members)  11.6 us
    all_to_all x1, starting transfers between devices, local(): lax.all_to_all(request.reshape(n_devices, capacity), ('lat', 'lon'), spli...  10.4 us
  transfers between devices with their start and end apart: 7, of which 6 were waited for; matrix products, arithmetic and copies ran while one was open for 5% of the time, Pallas kernels for 0%

commit v1 on v0

v1 whole, which is shorter than its diff:
```python
import jax
import jax.numpy as jnp
from jax import lax
from jax.experimental import pallas as pl
from jax.experimental.pallas import tpu as pltpu
from jax.sharding import PartitionSpec as P

NS_ITERS = 4
TILE = 32


def neighbours(block, axis, periodic):
    count = lax.axis_size(axis)
    forward = [(i, i + 1) for i in range(count - 1)]
    if periodic:
        forward.append((count - 1, 0))
    backward = [(target, source) for source, target in forward]
    return lax.ppermute(block, axis, forward), block, lax.ppermute(block, axis, backward)


def split(a):
    high = a.astype(jnp.bfloat16)
    low = (a - high.astype(jnp.float32)).astype(jnp.bfloat16)
    return high, low


def product(a, b):
    (a_high, a_low), (b_high, b_low) = a, b
    small = jnp.dot(a_high, b_low, preferred_element_type=jnp.float32)
    small += jnp.dot(a_low, b_high, preferred_element_type=jnp.float32)
    return small + jnp.dot(a_high, b_high, preferred_element_type=jnp.float32)


def weights_kernel(slots, blocks, departs, out, held, sems):
    domains, rows, members = held.shape
    entries = sems.shape[0]
    list_len = entries // domains
    block_rows = rows // list_len

    def fetch(e):
        d, l = e // list_len, e % list_len
        return pltpu.make_async_copy(
            blocks.at[slots[e]],
            held.at[d, pl.ds(pl.multiple_of(l * block_rows, block_rows), block_rows), :],
            sems.at[e],
        )

    @pl.loop(0, entries)
    def _(e):
        fetch(e).start()

    @pl.loop(0, domains)
    def _(d):
        @pl.loop(0, list_len)
        def _(l):
            fetch(d * list_len + l).wait()

        listed = held[d]
        gram = lax.dot_general(
            listed, listed, (((0,), (0,)), ((), ())), preferred_element_type=jnp.float32
        )
        innov = jnp.dot(departs[d], listed, preferred_element_type=jnp.float32)
        innov = jnp.transpose(jnp.broadcast_to(innov[:1], (128, members)))
        row = lax.broadcasted_iota(jnp.int32, (members, members), 0)
        column = lax.broadcasted_iota(jnp.int32, (members, members), 1)
        identity = (row == column).astype(jnp.float32)
        system = (members - 1.0) * identity + gram
        scale = jnp.sqrt(jnp.sum(system * system, keepdims=True))
        approx = system / scale
        root = None
        for sweep in range(NS_ITERS):
            approx_parts = split(approx)
            if root is None:
                factor = 1.5 * identity - 0.5 * approx
                factor_parts = split(factor)
                root = factor
            else:
                root_parts = split(root)
                factor = 1.5 * identity - 0.5 * product(root_parts, approx_parts)
                factor_parts = split(factor)
                root = product(factor_parts, root_parts)
            if sweep < NS_ITERS - 1:
                approx = product(approx_parts, factor_parts)
        root_parts = split(root)
        inner = product(root_parts, split(innov))
        mean_weight = product(root_parts, split(inner)) / scale
        gain = jnp.sqrt((members - 1.0) / scale)
        for part in range(members // 128):
            lanes = slice(part * 128, part * 128 + 128)
            out[d, :, lanes] = (gain * root[:, lanes] + mean_weight).astype(jnp.bfloat16)


def make_weights(slots, blocks, departs, domains):
    entries = slots.shape[0]
    block_rows, members = blocks.shape[1:]
    rows = entries // domains * block_rows
    wide = jnp.broadcast_to(departs.reshape(domains, 1, rows), (domains, 16, rows))
    return pl.pallas_call(
        weights_kernel,
        out_shape=jax.ShapeDtypeStruct((domains, members, members), jnp.bfloat16),
        grid_spec=pltpu.PrefetchScalarGridSpec(
            num_scalar_prefetch=1,
            grid=(),
            in_specs=[
                pl.BlockSpec(memory_space=pl.ANY),
                pl.BlockSpec(memory_space=pltpu.VMEM),
            ],
            out_specs=pl.BlockSpec(memory_space=pltpu.VMEM),
            scratch_shapes=[
                pltpu.VMEM((domains, rows, members), jnp.bfloat16),
                pltpu.SemaphoreType.DMA((entries,)),
            ],
        ),
        compiler_params=pltpu.CompilerParams(vmem_limit_bytes=40 << 20),
        name="weights",
    )(slots, blocks, wide)


def interp_kernel(position, low, middle, high, perturbed, terms, out, tiles, sems):
    step = pl.program_id(0)
    levels, columns, members = perturbed.shape
    near = middle.shape[0]
    per_step = columns // TILE
    n_interp = terms.shape[1] - levels

    @pl.when(step == 0)
    def _():
        copies = [
            pltpu.make_async_copy(ref, tiles.at[pl.ds(i * near, near)], sems.at[i])
            for i, ref in enumerate((low, middle, high))
        ]
        for copy in copies:
            copy.start()
        for copy in copies:
            copy.wait()

    for t in range(per_step):
        cols = slice(t * TILE, t * TILE + TILE)
        x = perturbed[:, cols, :].reshape(levels * TILE, members)
        total = None
        for corner in range(n_interp):
            chosen = tiles[position[(step * per_step + t) * n_interp + corner]]
            moved = jnp.dot(x, chosen, preferred_element_type=jnp.float32)
            moved = moved.reshape(levels, TILE, members)
            coef = jnp.broadcast_to(
                terms[cols, levels + corner : levels + corner + 1], (TILE, members)
            )
            total = coef[None] * moved if total is None else total + coef[None] * moved
        for level in range(levels):
            mean = jnp.broadcast_to(terms[cols, level : level + 1], (TILE, members))
            out[level, cols, :] = (mean + total[level]).astype(jnp.bfloat16)


def interpolate(position, near, state_pert, terms, per_step):
    levels, cols_here, members = state_pert.shape
    columns = per_step * TILE
    return pl.pallas_call(
        interp_kernel,
        out_shape=jax.ShapeDtypeStruct(state_pert.shape, jnp.bfloat16),
        grid_spec=pltpu.PrefetchScalarGridSpec(
            num_scalar_prefetch=1,
            grid=(cols_here // columns,),
            in_specs=[pl.BlockSpec(memory_space=pl.ANY)] * 3
            + [
                pl.BlockSpec((levels, columns, members), lambda i, p: (0, i, 0)),
                pl.BlockSpec((columns, terms.shape[1]), lambda i, p: (i, 0)),
            ],
            out_specs=pl.BlockSpec((levels, columns, members), lambda i, p: (0, i, 0)),
            scratch_shapes=[
                pltpu.VMEM((3 * near[1].shape[0], members, members), jnp.bfloat16),
                pltpu.SemaphoreType.DMA((3,)),
            ],
        ),
        compiler_params=pltpu.CompilerParams(vmem_limit_bytes=40 << 20),
        name="interp",
    )(position, *near, state_pert, terms)


def local(
    obs_pert, obs_dep, valid_rows, local_lists, state_mean, state_pert, interp_lists, interp_coef
):
    n_devices = lax.axis_size(("lat", "lon"))
    n_lon = lax.axis_size("lon")
    blocks_here, block_rows, members = obs_pert.shape
    keep = jnp.arange(block_rows)[None, :] < valid_rows[:, None]
    masked_pert = jnp.where(keep[:, :, None], obs_pert, jnp.zeros((), jnp.bfloat16))
    masked_dep = jnp.where(keep, obs_dep, jnp.zeros((), jnp.bfloat16))
    capacity = 2 * max(1, 64 // n_devices)
    domains_here, list_len = local_lists.shape
    entries = local_lists.reshape(-1)
    source = entries // blocks_here
    local_index = entries % blocks_here
    onehot = (source[:, None] == jnp.arange(n_devices, dtype=jnp.int32)[None, :]).astype(jnp.int32)
    earlier = jnp.cumsum(onehot, axis=0) - onehot
    slot = jnp.sum(earlier * onehot, axis=1)
    flat_slot = source * capacity + slot
    request = jnp.zeros((n_devices * capacity,), jnp.int32).at[flat_slot].set(local_index)
    asked = lax.all_to_all(
        request.reshape(n_devices, capacity),
        ("lat", "lon"),
        split_axis=0,
        concat_axis=0,
        tiled=True,
    ).reshape(-1)
    out_pert = masked_pert[asked].reshape(n_devices, capacity, block_rows, members)
    out_dep = masked_dep[asked].reshape(n_devices, capacity, block_rows)
    arrived = (
        lax.all_to_all(out_pert, ("lat", "lon"), split_axis=0, concat_axis=0, tiled=True),
        lax.all_to_all(out_dep, ("lat", "lon"), split_axis=0, concat_axis=0, tiled=True),
    )
    got_dep = arrived[1].reshape(-1, block_rows)[flat_slot]
    weights = make_weights(
        flat_slot, arrived[0].reshape(-1, block_rows, members), got_dep, domains_here
    )
    beside = jnp.concatenate(neighbours(weights, "lon", True), axis=0)
    near = neighbours(beside, "lat", False)
    owner = interp_lists // domains_here
    within = interp_lists % domains_here
    lat_step = owner // n_lon - lax.axis_index("lat")
    lon_step = (owner % n_lon - lax.axis_index("lon") + 1) % n_lon - 1
    position = ((lat_step + 1) * 3 + lon_step + 1) * domains_here + within
    terms = jnp.concatenate([state_mean, interp_coef], axis=0).T
    return interpolate(position.reshape(-1), near, state_pert, terms, 4)


def solution(mesh):
    in_specs = (
        P(("lat", "lon"), None, None),
        P(("lat", "lon"), None),
        P(("lat", "lon")),
        P(("lat", "lon"), None),
        P(None, ("lat", "lon")),
        P(None, ("lat", "lon"), None),
        P(("lat", "lon"), None),
        P(None, ("lat", "lon")),
    )
    out_specs = P(None, ("lat", "lon"), None)
    return jax.shard_map(local, mesh=mesh, in_specs=in_specs, out_specs=out_specs, check_vma=False)
```

time: 475 us -> 379 us (0.80)
  matrix products: 87 us -> 0 us
  Pallas kernels: 0 us -> 35 us
  local copies, waits for them, and re-layouts: 56.4 us -> 21.6 us
  other arithmetic: 13.6 us -> 8.22 us
    dot_general x19 -> x0, matrix products: 87 us -> none  [the longest x4 64.2 us: local(): jnp.einsum('ltci,tij->ltcj', perturbed, chosen[:, corner], preferred_elem...]
    pallas_call x0 -> x2, Pallas kernels: none -> 35 us  [the longest x1 19.1 us: make_weights(): pl.pallas_call(weights_kernel, out_shape=jax.ShapeDtypeStruct((domains, m...]
    gather x3 -> x1, local copies, waits for them, and re-layouts: 28.8 us -> 0.68 us  [local(): got_dep = arrived[1].reshape(-1, block_rows)[flat_slot]]
    convert_element_type x1 -> x0, local copies, waits for them, and re-layouts: 8.18 us -> none  [local(): return total.reshape(levels, cols_here, members).astype(jnp.bfloat16)]
    concatenate x2, other arithmetic: 5.14 us -> 0.18 us  [the longest x1 0.17 us: local(): beside = jnp.concatenate(neighbours(weights, 'lon', True), axis=0)]
where the time goes in v1:
time: 379 us; the launch traced here: 376 us
  waiting for transfers between devices  269 us (71%)
  starting transfers between devices  42.4 us (11%)
  Pallas kernels  35 us (9%)
  local copies, waits for them, and re-layouts  21.6 us (6%)
  other arithmetic  8.22 us (2%)
    all_to_all x1, waiting for transfers between devices, local(): lax.all_to_all(out_pert, ('lat', 'lon'), split_axis=0, concat_axis=0, til...  231 us
    pallas_call x1, Pallas kernels, make_weights(): pl.pallas_call(weights_kernel, out_shape=jax.ShapeDtypeStruct((domains, m...  19.1 us
    ppermute x2, waiting for transfers between devices, neighbours(): lax.ppermute(block, axis, forward)  17.8 us
    pallas_call x1, Pallas kernels, interpolate(): pl.pallas_call(interp_kernel, out_shape=jax.ShapeDtypeStruct(state_pert.s...  15.9 us
    ppermute x2, waiting for transfers between devices, neighbours(): lax.ppermute(block, axis, backward)  13 us
    ppermute x2, starting transfers between devices, neighbours(): lax.ppermute(block, axis, backward)  12 us
    gather x1, local copies, waits for them, and re-layouts, local(): masked_pert[asked].reshape(n_devices, capacity, block_rows, members)  11.6 us
    all_to_all x1, starting transfers between devices, local(): lax.all_to_all(request.reshape(n_devices, capacity), ('lat', 'lon'), spli...  10.4 us
  transfers between devices with their start and end apart: 7, of which 6 were waited for; matrix products, arithmetic and copies ran while one was open for 5% of the time, Pallas kernels for 0%

profile of v1, /device:TPU:10, one launch (start us, length us, event | category | flops | bytes accessed | tf_op | source)
XLA Modules:
  0.0 376.0 jit_solution(13248077694259896617)
XLA Ops:
  0.0 0.8 reshape.178
  0.8 0.8 reshape.179
  1.6 0.1 reduce_window_sum.11
  1.8 0.2 select_reduce_fusion
  2.0 0.9 scatter_custom_fusion
  2.8 0.8 all_to_all.12
  3.6 10.4 %all-to-all-start = ((s32[128,1,2]{2,1,0:T(1,128)}), s32[128,1,2]{2,1,0:T(1,128)S(1)}, u32[]{:S(2)}, u32[]{:S(2)}) async-start(s32[128,1,2]{2,1,0:T(1,128)} %bitcast.2), calls=%async_computation | async-start | bytes 131072 | tf_op jit(solution)/shard_map/all_to_all | solution.py:198
  14.0 0.8 broadcast_select_fusion.1
  14.8 0.7 iota_compare_fusion.1
  15.6 6.7 %all-to-all-done = s32[128,1,2]{2,1,0:T(1,128)S(1)} async-done(((s32[128,1,2]{2,1,0:T(1,128)}), s32[128,1,2]{2,1,0:T(1,128)S(1)}, u32[]{:S(2)}, u32[]{:S(2)}) %all-to-all-start) | async-done | bytes 1056 | tf_op jit(solution)/shard_map/all_to_all | solution.py:198
  22.3 0.5 broadcast.216
  22.8 0.8 reduce.3
  23.6 0.1 reshape.180
  23.8 1.5 gather_fusion.1
  25.2 5.8 %all-to-all-start.2 = ((bf16[128,2,128]{2,1,0:T(2,128)(2,1)}), bf16[128,2,128]{2,1,0:T(2,128)(2,1)S(1)}, u32[]{:S(2)}, u32[]{:S(2)}) async-start(bf16[128,2,128]{2,1,0:T(2,128)(2,1)} %bitcast.6), calls=%async_computation.2 | async-start | bytes 131072 | tf_op jit(solution)/shard_map/all_to_all | solution.py:209
  31.0 5.2 %broadcast_select_fusion = bf16[64,128,256]{2,1,0:T(8,128)(2,1)} fusion(bf16[64,128,256]{2,1,0:T(8,128)(2,1)} %param.8, pred[64,128]{1,0:T(8,128)(4,1)S(1)} %iota_compare_fusion.1), kind=kLoop, calls=%fused_computation.4 | loop fusion | flops 2097152 | bytes 8396800 | tf_op jit(solution)/shard_map/jit(_where)/select_n | solution.py:186
  36.3 11.6 %gather_fusion = bf16[256,128,256]{2,1,0:T(8,128)(2,1)} fusion(bf16[64,128,256]{2,1,0:T(8,128)(2,1)} %broadcast_select_fusion, s32[1024]{0:T(1024)S(1)} %pad_clamp_fusion.1), kind=kCustom, calls=%fused_computation | custom fusion | bytes 33555456 | tf_op jit(solution)/shard_map/gather | solution.py:205
  47.8 10.2 %all-to-all-start.1 = ((bf16[128,2,128,256]{3,2,1,0:T(8,128)(2,1)}), bf16[128,2,128,256]{3,2,1,0:T(8,128)(2,1)}, u32[]{:S(2)}, u32[]{:S(2)}) async-start(bf16[128,2,128,256]{3,2,1,0:T(8,128)(2,1)} %bitcast.14), calls=%async_computation.1 | async-start | bytes 33554432 | tf_op jit(solution)/shard_map/all_to_all | solution.py:208
  58.1 0.7 gather_fusion.2
  58.8 231.2 %all-to-all-done.1 = bf16[128,2,128,256]{3,2,1,0:T(8,128)(2,1)} async-done(((bf16[128,2,128,256]{3,2,1,0:T(8,128)(2,1)}), bf16[128,2,128,256]{3,2,1,0:T(8,128)(2,1)}, u32[]{:S(2)}, u32[]{:S(2)}) %all-to-all-start.1) | async-done | bytes 16777248 | tf_op jit(solution)/shard_map/all_to_all | solution.py:208
  290.1 19.1 %weights.1 = bf16[4,256,256]{2,1,0:T(8,128)(2,1)S(1)} custom-call(s32[96]{0:T(128)S(1)} %multiply_add_fusion.slots, bf16[256,128,256]{2,1,0:T(8,128)(2,1)} %bitcast.5.blocks, bf16[4,16,3072]{2,1,0:T(8,128)(2,1)S(1)} %broadcast_in_dim.36.departs), custom_call_target="tpu_custom_call" | custom-call | tf_op jit(solution)/shard_map/weights/pallas_call | solution.py:98
  309.2 2.0 collective-permute-start
  311.2 11.3 %collective-permute-done.1 = bf16[4,256,256]{2,1,0:T(8,128)(2,1)S(1)} collective-permute-done((bf16[4,256,256]{2,1,0:T(8,128)(2,1)S(1)}, bf16[4,256,256]{2,1,0:T(8,128)(2,1)S(1)}, u32[]{:S(2)}, u32[]{:S(2)}) %collective-permute-start.1) | collective-permute-done | bytes 524320 | tf_op jit(solution)/shard_map/ppermute | solution.py:18
  322.6 2.2 collective-permute-done
  324.8 0.2 pad_maximum_fusion.middle
  325.0 1.9 collective-permute-start.2
  326.9 11.9 %collective-permute-start.3 = (bf16[12,256,256]{2,1,0:T(8,128)(2,1)S(1)}, bf16[12,256,256]{2,1,0:T(8,128)(2,1)}, u32[]{:S(2)}, u32[]{:S(2)}) collective-permute-start(bf16[12,256,256]{2,1,0:T(8,128)(2,1)S(1)} %pad_maximum_fusion.middle), channel_id=1, source_target_pairs={{16,0},{32,16},{48,32},{64,48},{80,64},{96,80},{112,96},{17,1},{33... | collective-permute-start | bytes 4718600 | tf_op jit(solution)/shard_map/ppermute | solution.py:18
  339.1 0.4 copy.16
  339.5 15.6 %collective-permute-done.2.low = bf16[12,256,256]{2,1,0:T(8,128)(2,1)} collective-permute-done((bf16[12,256,256]{2,1,0:T(8,128)(2,1)S(1)}, bf16[12,256,256]{2,1,0:T(8,128)(2,1)}, u32[]{:S(2)}, u32[]{:S(2)}) %collective-permute-start.2) | collective-permute-done | bytes 1572896 | tf_op jit(solution)/shard_map/ppermute | solution.py:18
  355.1 1.7 collective-permute-done.3.high
  356.7 3.4 copy-done
  360.1 15.9 %interp.1 = bf16[8,2048,256]{2,1,0:T(8,128)(2,1)} custom-call(s32[256]{0:T(256)S(1)} %reshape.177.position, bf16[12,256,256]{2,1,0:T(8,128)(2,1)} %collective-permute-done.2.low, bf16[12,256,256]{2,1,0:T(8,128)(2,1)S(1)} %pad_maximum_fusion.middle, bf16[12,256,256]{2,1,0:T(8,128)(2,1)} %collective-permute-done.3.high, bf16[8,2048,256]{2,1,0:T(8,128)(2,1)S(1)} %copy-done, ...), custom_call_target="tpu_custom_call" | custom-call | tf_op jit(solution)/shard_map/interp/pallas_call | solution.py:157
  (22 shorter events, 0.5 us)
Async XLA Ops:
  3.6 18.6 %all-to-all-start = ((s32[128,1,2]{2,1,0:T(1,128)}), s32[128,1,2]{2,1,0:T(1,128)S(1)}, u32[]{:S(2)}, u32[]{:S(2)}) async-start(s32[128,1,2]{2,1,0:T(1,128)} %bitcast.2), calls=%async_computation | async-start | bytes 131072 | tf_op jit(solution)/shard_map/all_to_all | solution.py:198
  25.2 22.6 %all-to-all-start.2 = ((bf16[128,2,128]{2,1,0:T(2,128)(2,1)}), bf16[128,2,128]{2,1,0:T(2,128)(2,1)S(1)}, u32[]{:S(2)}, u32[]{:S(2)}) async-start(bf16[128,2,128]{2,1,0:T(2,128)(2,1)} %bitcast.6), calls=%async_computation.2 | async-start | bytes 131072 | tf_op jit(solution)/shard_map/all_to_all | solution.py:209
  47.8 242.2 %all-to-all-start.1 = ((bf16[128,2,128,256]{3,2,1,0:T(8,128)(2,1)}), bf16[128,2,128,256]{3,2,1,0:T(8,128)(2,1)}, u32[]{:S(2)}, u32[]{:S(2)}) async-start(bf16[128,2,128,256]{3,2,1,0:T(8,128)(2,1)} %bitcast.14), calls=%async_computation.1 | async-start | bytes 33554432 | tf_op jit(solution)/shard_map/all_to_all | solution.py:208
  290.1 48.8 %copy-start.3 = (s32[64,4]{0,1:T(4,128)S(1)}, s32[64,4]{0,1:T(4,128)}, u32[]{:S(2)}) copy-start(s32[64,4]{0,1:T(4,128)} %param.14) | copy-start | bytes 3076
  290.1 49.0 %copy-start.1 = (f32[8,2048]{1,0:T(8,128)S(1)}, f32[8,2048]{1,0:T(8,128)}, u32[]{:S(2)}) copy-start(f32[8,2048]{1,0:T(8,128)} %param.12) | copy-start | bytes 196612
  290.1 49.0 %copy-start.2 = (f32[4,2048]{1,0:T(4,128)S(1)}, f32[4,2048]{1,0:T(4,128)}, u32[]{:S(2)}) copy-start(f32[4,2048]{1,0:T(4,128)} %param.15) | copy-start | bytes 98308
  309.1 13.4 %collective-permute-start.1 = (bf16[4,256,256]{2,1,0:T(8,128)(2,1)S(1)}, bf16[4,256,256]{2,1,0:T(8,128)(2,1)S(1)}, u32[]{:S(2)}, u32[]{:S(2)}) collective-permute-start(bf16[4,256,256]{2,1,0:T(8,128)(2,1)S(1)} %weights.1), channel_id=1, source_target_pairs={{1,0},{2,1},{3,2},{4,3},{5,4},{6,5},{7,6},{8,7},{9,8},{10,9},{11,1... | collective-permute-start | bytes 1572872 | tf_op jit(solution)/shard_map/ppermute | solution.py:18
  309.2 15.5 %collective-permute-start = (bf16[4,256,256]{2,1,0:T(8,128)(2,1)S(1)}, bf16[4,256,256]{2,1,0:T(8,128)(2,1)S(1)}, u32[]{:S(2)}, u32[]{:S(2)}) collective-permute-start(bf16[4,256,256]{2,1,0:T(8,128)(2,1)S(1)} %weights.1), channel_id=1, source_target_pairs={{0,1},{1,2},{2,3},{3,4},{4,5},{5,6},{6,7},{7,8},{8,9},{9,10},{10,1... | collective-permute-start | bytes 1572872 | tf_op jit(solution)/shard_map/ppermute | solution.py:18
  325.0 30.1 %collective-permute-start.2 = (bf16[12,256,256]{2,1,0:T(8,128)(2,1)S(1)}, bf16[12,256,256]{2,1,0:T(8,128)(2,1)}, u32[]{:S(2)}, u32[]{:S(2)}) collective-permute-start(bf16[12,256,256]{2,1,0:T(8,128)(2,1)S(1)} %pad_maximum_fusion.middle), channel_id=1, source_target_pairs={{0,16},{16,32},{32,48},{48,64},{64,80},{80,96},{96,112},{1,17},{17... | collective-permute-start | bytes 4718600 | tf_op jit(solution)/shard_map/ppermute | solution.py:18
  326.9 29.8 %collective-permute-start.3 = (bf16[12,256,256]{2,1,0:T(8,128)(2,1)S(1)}, bf16[12,256,256]{2,1,0:T(8,128)(2,1)}, u32[]{:S(2)}, u32[]{:S(2)}) collective-permute-start(bf16[12,256,256]{2,1,0:T(8,128)(2,1)S(1)} %pad_maximum_fusion.middle), channel_id=1, source_target_pairs={{16,0},{32,16},{48,32},{64,48},{80,64},{96,80},{112,96},{17,1},{33... | collective-permute-start | bytes 4718600 | tf_op jit(solution)/shard_map/ppermute | solution.py:18
  356.7 3.4 copy-start
